TPU v7x, 32 devices: a whole 2x2x4 slice. The times are simulated.
32 devices in a mesh: rows: 16 (over z, x, core), cols: 2 (over y).
Axes of the slice: x: 2, y: 2, z: 4, core: 2. Of those that a mesh axis runs over, the one named last changes fastest.
Arguments:
- kernel: float32 [16384, 1536], P('rows', 'cols'), may hold values from -0.15625 to 0.15625
- row_orbitals: float32 [16384, 512], P('rows', 'cols'), may hold values from -1.5 to 1.5
- col_orbitals: float32 [1536, 512], P('cols', 'rows'), may hold values from -1.5 to 1.5
- col_vectors: float32 [1536, 512], P('cols', 'rows'), may hold values from -6 to 6
Outputs:
- exchange: float32 [512, 16384], P('cols', 'rows')
All inputs are finite; a program needn't handle non-finite values.
Results may differ from a plain program's by a relative error of at most 0.0003.
Values sent between devices are 32-bit elements; how exact they have to be, the bound alone decides.
A program may use at most 64 MiB of HBM per device.

v0:
```python
import jax
import jax.numpy as jnp
from jax import lax
from jax.sharding import PartitionSpec as P


def body(kernel, row_orbitals, col_orbitals, col_vectors):
    full_rows = lax.all_gather(row_orbitals, "cols", axis=1, tiled=True)
    full_cols = lax.all_gather(col_orbitals, "rows", axis=1, tiled=True)
    full_vecs = lax.all_gather(col_vectors, "rows", axis=1, tiled=True)
    gram = jnp.dot(
        full_rows, full_cols.T, precision=lax.Precision.HIGHEST, preferred_element_type=jnp.float32
    )
    weighted = kernel * gram
    return lax.psum_scatter(
        -jnp.dot(
            full_vecs.T,
            weighted.T,
            precision=lax.Precision.HIGHEST,
            preferred_element_type=jnp.float32,
        ),
        "cols",
        scatter_dimension=0,
        tiled=True,
    )


def solution(mesh):
    in_specs = (P("rows", "cols"), P("rows", "cols"), P("cols", "rows"), P("cols", "rows"))
    out_specs = P("cols", "rows")
    return jax.shard_map(body, mesh=mesh, in_specs=in_specs, out_specs=out_specs, check_vma=False)
```

profile of v0, /device:TPU:0, one launch (start us, length us, event | category | flops | bytes accessed | tf_op | source)
XLA Modules:
  0.0 175.4 jit_solution(11052527146017626073)
XLA Ops:
  6.5 0.0 all-gather.4.cloned.1.call-start
  6.5 0.7 all-gather.4.cloned.1.call-update
  7.3 0.0 all-gather.6.cloned.1.call-start
  7.3 0.7 all-gather.6.cloned.1.call-update
  8.0 0.0 all-gather.8.cloned.1.call-start
  8.1 0.7 all-gather.8.cloned.1.call-update
  8.7 0.0 reduce-scatter.2.cloned.1.call-start
  8.8 35.9 %all-gather.4.cloned.1.call-done = f32[1024,512]{1,0:T(8,128)} async-done(((f32[1024,256]{1,0:T(8,128)}), f32[1024,512]{1,0:T(8,128)}) %all-gather.4.cloned.1.call-update) | async-done | bytes 2097168 | tf_op jit(solution)/shard_map/all_gather | solution.py:8
  44.7 41.9 %all-gather.6.cloned.1.call-done = f32[768,512]{0,1:T(8,128)} async-done(((f32[768,32]{0,1:T(8,128)}), f32[768,512]{0,1:T(8,128)}) %all-gather.6.cloned.1.call-update) | async-done | bytes 1572880 | tf_op jit(solution)/shard_map/all_gather | solution.py:9
  86.6 7.2 %fusion.4 = f32[1024,768]{1,0:T(8,128)S(1)} fusion(f32[1024,512]{1,0:T(8,128)} %all-gather.4.cloned.1.call-done, f32[768,512]{0,1:T(8,128)} %all-gather.6.cloned.1.call-done), kind=kOutput, calls=%fused_computation.3 | convolution fusion | flops 4831838208 | bytes 6815744 | tf_op jit(solution)/shard_map/dot_general | solution.py:11
  93.9 33.4 %all-gather.8.cloned.1.call-done = f32[768,512]{0,1:T(8,128)} async-done(((f32[768,32]{0,1:T(8,128)}), f32[768,512]{0,1:T(8,128)}) %all-gather.8.cloned.1.call-update) | async-done | bytes 1572880 | tf_op jit(solution)/shard_map/all_gather | solution.py:10
  127.3 8.3 %negate_bitcast_fusion = f32[512,1024]{0,1:T(8,128)} fusion(f32[768,512]{0,1:T(8,128)} %all-gather.8.cloned.1.call-done, f32[1024,768]{1,0:T(8,128)} %param.4, f32[1024,768]{1,0:T(8,128)S(1)} %fusion.4), kind=kOutput, calls=%fused_computation.2 | convolution fusion | flops 4833148928 | bytes 9961472 | tf_op jit(solution)/shard_map/dot_general | solution.py:16
  135.6 0.0 reduce-scatter.2.cloned.1.call-update
  135.6 30.8 %reduce-scatter.2.cloned.1.call-done = f32[256,1024]{0,1:T(8,128)} async-done(((f32[512,1024]{0,1:T(8,128)}), f32[256,1024]{0,1:T(8,128)}) %reduce-scatter.2.cloned.1.call-update) | async-done | bytes 1048592 | tf_op jit(solution)/shard_map/reduce_scatter | solution.py:15
  166.4 2.5 %copy.5 = f32[256,1024]{1,0:T(8,128)} copy(f32[256,1024]{0,1:T(8,128)} %reduce-scatter.2.cloned.1.call-done) | data formatting | bytes 2097152 | tf_op jit(solution)/shard_map/reduce_scatter | solution.py:15
Async XLA Ops:
  6.5 38.2 %all-gather.4.cloned.1.call-start = ((), (), s32[]{:S(2)}) async-start(), calls=%async_computation.1 | async-start | bytes 3145728 | tf_op jit(solution)/shard_map/all_gather | solution.py:8
  7.3 79.4 %all-gather.6.cloned.1.call-start = ((), (), s32[]{:S(2)}) async-start(), calls=%async_computation.2 | async-start | bytes 1671168 | tf_op jit(solution)/shard_map/all_gather | solution.py:9
  8.0 119.3 %all-gather.8.cloned.1.call-start = ((), (), s32[]{:S(2)}) async-start(), calls=%async_computation.3 | async-start | bytes 1671168 | tf_op jit(solution)/shard_map/all_gather | solution.py:10
  8.7 157.6 %reduce-scatter.2.cloned.1.call-start = ((), (), s32[]{:S(2)}) async-start(), calls=%async_computation.4 | async-start | bytes 3145728 | tf_op jit(solution)/shard_map/reduce_scatter | solution.py:15
Sparse Core Ops, SparseCore 0:
  8.9 35.8 all-gather.3
  47.0 39.5 all-gather.5
  88.9 38.2 all-gather.7
  135.7 30.6 reduce-scatter.1
where the time goes:
time: 176 us; the launch traced here: 175 us
  waiting for transfers between devices  144 us (82%)
  matrix products  15.6 us (9%)
  between operations  13.1 us (7%)
  local copies, waits for them, and re-layouts  2.53 us (1%)
    all_gather x1, waiting for transfers between devices, body(): full_cols = lax.all_gather(col_orbitals, 'rows', axis=1, tiled=True)  41.9 us
    all_gather x1, waiting for transfers between devices, body(): full_rows = lax.all_gather(row_orbitals, 'cols', axis=1, tiled=True)  35.9 us
    all_gather x1, waiting for transfers between devices, body(): full_vecs = lax.all_gather(col_vectors, 'rows', axis=1, tiled=True)  33.4 us
    reduce_scatter x1, waiting for transfers between devices, body(): lax.psum_scatter(-jnp.dot(full_vecs.T, weighted.T, precision=lax.Precisio...  30.8 us
    dot_general x1, matrix products, body(): jnp.dot(full_vecs.T, weighted.T, precision=lax.Precision.HIGHEST, preferr...  8.31 us
    dot_general x1, matrix products, body(): jnp.dot(full_rows, full_cols.T, precision=lax.Precision.HIGHEST, preferre...  7.25 us
  transfers between devices with their start and end apart: 4, of which 4 were waited for; matrix products, arithmetic and copies ran while one was open for 4% of the time, Pallas kernels for 0%

commit v1 on v0

--- a/solution.py
+++ b/solution.py
@@ -7,7 +7,15 @@
 def body(kernel, row_orbitals, col_orbitals, col_vectors):
     full_rows = lax.all_gather(row_orbitals, "cols", axis=1, tiled=True)
     full_cols = lax.all_gather(col_orbitals, "rows", axis=1, tiled=True)
-    full_vecs = lax.all_gather(col_vectors, "rows", axis=1, tiled=True)
+    n_shards = lax.axis_size("rows")
+    y = col_vectors
+    buffer = [y]
+    now = sorted(((it, (it + 1) % n_shards) for it in range(n_shards)))
+    for d in range(1, n_shards):
+        y = lax.ppermute(y, "rows", now)
+        buffer.insert(0, y)
+    s_next = jnp.concatenate(buffer, axis=1)
+    full_vecs = jnp.roll(s_next, (lax.axis_index("rows") + 1) * col_vectors.shape[1], axis=1)
     gram = jnp.dot(
         full_rows, full_cols.T, precision=lax.Precision.HIGHEST, preferred_element_type=jnp.float32
     )

time: 176 us -> 197 us (1.12)
  local copies, waits for them, and re-layouts: 2.53 us -> 20.5 us
  waiting for transfers between devices: 144 us -> 147 us
    ppermute x0 -> x15, waiting for transfers between devices: none -> 102 us  [body(): y = lax.ppermute(y, 'rows', now)]
    all_gather x1, waiting for transfers between devices: 35.9 us -> 0.01 us  [body(): full_rows = lax.all_gather(row_orbitals, 'cols', axis=1, tiled=True)]
    all_gather x1 -> x0, waiting for transfers between devices: 33.4 us -> none  [body(): full_vecs = lax.all_gather(col_vectors, 'rows', axis=1, tiled=True)]
    all_gather x1, waiting for transfers between devices: 41.9 us -> 14.2 us  [body(): full_cols = lax.all_gather(col_orbitals, 'rows', axis=1, tiled=True)]
    unnamed x0 -> x35, local copies, waits for them, and re-layouts: none -> 19.8 us
    reduce_scatter x1 -> x0, local copies, waits for them, and re-layouts: 2.53 us -> none  [body(): lax.psum_scatter(-jnp.dot(full_vecs.T, weighted.T, precision=lax.Precisio...]
  transfers between devices with their start and end apart: 4 -> 18, of which waited for: 4 -> 17; matrix products, arithmetic and copies ran while one was open for 4% -> 10% of each run, Pallas kernels for 0% -> 0%
where the time goes in v1:
time: 197 us
  waiting for transfers between devices  147 us (75%)
  local copies, waits for them, and re-layouts  20.5 us (10%)
  matrix products  15.6 us (8%)
  between operations  13.2 us (7%)
    ppermute x15, waiting for transfers between devices, body(): y = lax.ppermute(y, 'rows', now)  102 us
    reduce_scatter x1, waiting for transfers between devices, body(): lax.psum_scatter(-jnp.dot(full_vecs.T, weighted.T, precision=lax.Precisio...  30.8 us
    unnamed x35, local copies, waits for them, and re-layouts  19.8 us
    all_gather x1, waiting for transfers between devices, body(): full_cols = lax.all_gather(col_orbitals, 'rows', axis=1, tiled=True)  14.2 us
    dot_general x1, matrix products, body(): jnp.dot(full_vecs.T, weighted.T, precision=lax.Precision.HIGHEST, preferr...  8.05 us
    dot_general x1, matrix products, body(): jnp.dot(full_rows, full_cols.T, precision=lax.Precision.HIGHEST, preferre...  7.54 us
  transfers between devices with their start and end apart: 18, of which 17 were waited for; matrix products, arithmetic and copies ran while one was open for 10% of the time, Pallas kernels for 0%

profile of v1, /device:TPU:0, one launch (start us, length us, event | category | flops | bytes accessed | tf_op | source)
XLA Modules:
  0.0 197.3 jit_solution(2809033979335039797)
XLA Ops:
  6.5 0.7 all-gather.3.cloned.1.call-update
  7.8 7.5 %collective-permute-done = f32[768,32]{0,1:T(8,128)S(1)} collective-permute-done((f32[768,32]{0,1:T(8,128)}, f32[768,32]{0,1:T(8,128)S(1)}, u32[]{:S(2)}, u32[]{:S(2)}) %collective-permute-start) | collective-permute-done | bytes 98336 | tf_op jit(solution)/shard_map/ppermute | solution.py:15
  15.3 6.7 %collective-permute-done.1 = f32[768,32]{0,1:T(8,128)S(1)} collective-permute-done((f32[768,32]{0,1:T(8,128)S(1)}, f32[768,32]{0,1:T(8,128)S(1)}, u32[]{:S(2)}, u32[]{:S(2)}) %collective-permute-start.1) | collective-permute-done | bytes 98336 | tf_op jit(solution)/shard_map/ppermute | solution.py:15
  22.1 6.7 %collective-permute-done.2 = f32[768,32]{0,1:T(8,128)S(1)} collective-permute-done((f32[768,32]{0,1:T(8,128)S(1)}, f32[768,32]{0,1:T(8,128)S(1)}, u32[]{:S(2)}, u32[]{:S(2)}) %collective-permute-start.2) | collective-permute-done | bytes 98336 | tf_op jit(solution)/shard_map/ppermute | solution.py:15
  28.8 6.7 %collective-permute-done.3 = f32[768,32]{0,1:T(8,128)S(1)} collective-permute-done((f32[768,32]{0,1:T(8,128)S(1)}, f32[768,32]{0,1:T(8,128)S(1)}, u32[]{:S(2)}, u32[]{:S(2)}) %collective-permute-start.3) | collective-permute-done | bytes 98336 | tf_op jit(solution)/shard_map/ppermute | solution.py:15
  35.5 6.7 %collective-permute-done.4 = f32[768,32]{0,1:T(8,128)S(1)} collective-permute-done((f32[768,32]{0,1:T(8,128)S(1)}, f32[768,32]{0,1:T(8,128)S(1)}, u32[]{:S(2)}, u32[]{:S(2)}) %collective-permute-start.4) | collective-permute-done | bytes 98336 | tf_op jit(solution)/shard_map/ppermute | solution.py:15
  42.3 6.7 %collective-permute-done.5 = f32[768,32]{0,1:T(8,128)S(1)} collective-permute-done((f32[768,32]{0,1:T(8,128)S(1)}, f32[768,32]{0,1:T(8,128)S(1)}, u32[]{:S(2)}, u32[]{:S(2)}) %collective-permute-start.5) | collective-permute-done | bytes 98336 | tf_op jit(solution)/shard_map/ppermute | solution.py:15
  49.0 6.7 %collective-permute-done.6 = f32[768,32]{0,1:T(8,128)S(1)} collective-permute-done((f32[768,32]{0,1:T(8,128)S(1)}, f32[768,32]{0,1:T(8,128)S(1)}, u32[]{:S(2)}, u32[]{:S(2)}) %collective-permute-start.6) | collective-permute-done | bytes 98336 | tf_op jit(solution)/shard_map/ppermute | solution.py:15
  55.8 6.7 %collective-permute-done.7 = f32[768,32]{0,1:T(8,128)S(1)} collective-permute-done((f32[768,32]{0,1:T(8,128)S(1)}, f32[768,32]{0,1:T(8,128)S(1)}, u32[]{:S(2)}, u32[]{:S(2)}) %collective-permute-start.7) | collective-permute-done | bytes 98336 | tf_op jit(solution)/shard_map/ppermute | solution.py:15
  62.5 6.7 %collective-permute-done.8 = f32[768,32]{0,1:T(8,128)S(1)} collective-permute-done((f32[768,32]{0,1:T(8,128)S(1)}, f32[768,32]{0,1:T(8,128)S(1)}, u32[]{:S(2)}, u32[]{:S(2)}) %collective-permute-start.8) | collective-permute-done | bytes 98336 | tf_op jit(solution)/shard_map/ppermute | solution.py:15
  69.2 6.7 %collective-permute-done.9 = f32[768,32]{0,1:T(8,128)S(1)} collective-permute-done((f32[768,32]{0,1:T(8,128)S(1)}, f32[768,32]{0,1:T(8,128)S(1)}, u32[]{:S(2)}, u32[]{:S(2)}) %collective-permute-start.9) | collective-permute-done | bytes 98336 | tf_op jit(solution)/shard_map/ppermute | solution.py:15
  76.0 6.7 %collective-permute-done.10 = f32[768,32]{0,1:T(8,128)S(1)} collective-permute-done((f32[768,32]{0,1:T(8,128)S(1)}, f32[768,32]{0,1:T(8,128)S(1)}, u32[]{:S(2)}, u32[]{:S(2)}) %collective-permute-start.10) | collective-permute-done | bytes 98336 | tf_op jit(solution)/shard_map/ppermute | solution.py:15
  82.7 6.7 %collective-permute-done.11 = f32[768,32]{0,1:T(8,128)S(1)} collective-permute-done((f32[768,32]{0,1:T(8,128)S(1)}, f32[768,32]{0,1:T(8,128)S(1)}, u32[]{:S(2)}, u32[]{:S(2)}) %collective-permute-start.11) | collective-permute-done | bytes 98336 | tf_op jit(solution)/shard_map/ppermute | solution.py:15
  89.5 6.7 %collective-permute-done.12 = f32[768,32]{0,1:T(8,128)S(1)} collective-permute-done((f32[768,32]{0,1:T(8,128)S(1)}, f32[768,32]{0,1:T(8,128)S(1)}, u32[]{:S(2)}, u32[]{:S(2)}) %collective-permute-start.12) | collective-permute-done | bytes 98336 | tf_op jit(solution)/shard_map/ppermute | solution.py:15
  96.2 6.7 %collective-permute-done.13 = f32[768,32]{0,1:T(8,128)S(1)} collective-permute-done((f32[768,32]{0,1:T(8,128)S(1)}, f32[768,32]{0,1:T(8,128)S(1)}, u32[]{:S(2)}, u32[]{:S(2)}) %collective-permute-start.13) | collective-permute-done | bytes 98336 | tf_op jit(solution)/shard_map/ppermute | solution.py:15
  103.0 6.6 %collective-permute-done.14 = f32[768,32]{0,1:T(8,128)S(1)} collective-permute-done((f32[768,32]{0,1:T(8,128)S(1)}, f32[768,32]{0,1:T(8,128)S(1)}, u32[]{:S(2)}, u32[]{:S(2)}) %collective-permute-start.14) | collective-permute-done | bytes 98336 | tf_op jit(solution)/shard_map/ppermute | solution.py:15
  110.9 0.6 constant_dynamic-update-slice_fusion.29
  113.5 0.6 constant_dynamic-update-slice_fusion.25
  114.8 0.6 constant_dynamic-update-slice_fusion.23
  116.1 0.6 constant_dynamic-update-slice_fusion.21
  116.7 0.6 constant_dynamic-update-slice_fusion.20
  118.6 0.6 constant_dynamic-update-slice_fusion.17
  119.9 0.6 constant_dynamic-update-slice_fusion.15
  121.8 0.6 constant_dynamic-update-slice_fusion.12
  122.5 0.6 constant_dynamic-update-slice_fusion.11
  123.7 0.6 constant_dynamic-update-slice_fusion.9
  125.0 0.6 constant_dynamic-update-slice_fusion.7
  129.5 0.7 constant_dynamic-update-slice_fusion
  130.1 14.2 %all-gather.5.cloned.1.call-done = f32[768,512]{0,1:T(8,128)} async-done(((f32[768,32]{0,1:T(8,128)}), f32[768,512]{0,1:T(8,128)}) %all-gather.5.cloned.1.call-update) | async-done | bytes 1572880 | tf_op jit(solution)/shard_map/all_gather | solution.py:9
  144.4 7.5 %fusion.7 = f32[1024,768]{1,0:T(8,128)S(1)} fusion(f32[1024,512]{1,0:T(8,128)} %all-gather.3.cloned.1.call-done, f32[768,512]{0,1:T(8,128)} %all-gather.5.cloned.1.call-done), kind=kOutput, calls=%fused_computation.37 | convolution fusion | flops 4831838208 | bytes 6815744 | tf_op jit(solution)/shard_map/dot_general | solution.py:19
  151.9 8.0 %fusion.2 = f32[512,1024]{1,0:T(8,128)} fusion(f32[1024,768]{1,0:T(8,128)S(1)} %copy-done, f32[1024,768]{1,0:T(8,128)S(1)} %fusion.7, f32[768,1024]{0,1:T(8,128)} %constant_dynamic-update-slice_fusion, s32[]{:T(128)S(6)} %select_n.14), kind=kOutput, calls=%fused_computation.2 | convolution fusion | flops 4833148928 | bytes 9961476 | tf_op jit(solution)/shard_map/dot_general | solution.py:24
  160.0 30.8 %reduce-scatter.2.cloned.1.call-done = f32[256,1024]{1,0:T(8,128)} async-done(((f32[512,1024]{1,0:T(8,128)}), f32[256,1024]{1,0:T(8,128)}) %reduce-scatter.2.cloned.1.call-update) | async-done | bytes 1048592 | tf_op jit(solution)/shard_map/reduce_scatter | solution.py:23
  (45 shorter events, 13.4 us)
Async XLA Ops:
  6.5 112.7 %copy-start.1 = (f32[768,32]{0,1:T(8,128)S(1)}, f32[768,32]{0,1:T(8,128)}, u32[]{:S(2)}) copy-start(f32[768,32]{0,1:T(8,128)} %param.7) | copy-start | bytes 294916
  6.5 123.6 %all-gather.3.cloned.1.call-start = ((), (), s32[]{:S(2)}) async-start(), calls=%async_computation.1 | async-start | bytes 3145728 | tf_op jit(solution)/shard_map/all_gather | solution.py:8
  7.3 137.1 %all-gather.5.cloned.1.call-start = ((), (), s32[]{:S(2)}) async-start(), calls=%async_computation.2 | async-start | bytes 1671168 | tf_op jit(solution)/shard_map/all_gather | solution.py:9
  7.3 8.0 %collective-permute-start = (f32[768,32]{0,1:T(8,128)}, f32[768,32]{0,1:T(8,128)S(1)}, u32[]{:S(2)}, u32[]{:S(2)}) collective-permute-start(f32[768,32]{0,1:T(8,128)} %param.7), channel_id=1, source_target_pairs={{0,2},{2,4},{4,6},{6,8},{8,10},{10,12},{12,14},{14,16},{16,18},{18... | collective-permute-start | bytes 294920 | tf_op jit(solution)/shard_map/ppermute | solution.py:15
  15.3 6.7 %collective-permute-start.1 = (f32[768,32]{0,1:T(8,128)S(1)}, f32[768,32]{0,1:T(8,128)S(1)}, u32[]{:S(2)}, u32[]{:S(2)}) collective-permute-start(f32[768,32]{0,1:T(8,128)S(1)} %collective-permute-done), channel_id=1, source_target_pairs={{0,2},{2,4},{4,6},{6,8},{8,10},{10,12},{12,14},{14,16},{16,18},{18... | collective-permute-start | bytes 294920 | tf_op jit(solution)/shard_map/ppermute | solution.py:15
  22.1 6.7 %collective-permute-start.2 = (f32[768,32]{0,1:T(8,128)S(1)}, f32[768,32]{0,1:T(8,128)S(1)}, u32[]{:S(2)}, u32[]{:S(2)}) collective-permute-start(f32[768,32]{0,1:T(8,128)S(1)} %collective-permute-done.1), channel_id=1, source_target_pairs={{0,2},{2,4},{4,6},{6,8},{8,10},{10,12},{12,14},{14,16},{16,18},{18... | collective-permute-start | bytes 294920 | tf_op jit(solution)/shard_map/ppermute | solution.py:15
  28.8 6.7 %collective-permute-start.3 = (f32[768,32]{0,1:T(8,128)S(1)}, f32[768,32]{0,1:T(8,128)S(1)}, u32[]{:S(2)}, u32[]{:S(2)}) collective-permute-start(f32[768,32]{0,1:T(8,128)S(1)} %collective-permute-done.2), channel_id=1, source_target_pairs={{0,2},{2,4},{4,6},{6,8},{8,10},{10,12},{12,14},{14,16},{16,18},{18... | collective-permute-start | bytes 294920 | tf_op jit(solution)/shard_map/ppermute | solution.py:15
  35.5 6.7 %collective-permute-start.4 = (f32[768,32]{0,1:T(8,128)S(1)}, f32[768,32]{0,1:T(8,128)S(1)}, u32[]{:S(2)}, u32[]{:S(2)}) collective-permute-start(f32[768,32]{0,1:T(8,128)S(1)} %collective-permute-done.3), channel_id=1, source_target_pairs={{0,2},{2,4},{4,6},{6,8},{8,10},{10,12},{12,14},{14,16},{16,18},{18... | collective-permute-start | bytes 294920 | tf_op jit(solution)/shard_map/ppermute | solution.py:15
  42.3 6.7 %collective-permute-start.5 = (f32[768,32]{0,1:T(8,128)S(1)}, f32[768,32]{0,1:T(8,128)S(1)}, u32[]{:S(2)}, u32[]{:S(2)}) collective-permute-start(f32[768,32]{0,1:T(8,128)S(1)} %collective-permute-done.4), channel_id=1, source_target_pairs={{0,2},{2,4},{4,6},{6,8},{8,10},{10,12},{12,14},{14,16},{16,18},{18... | collective-permute-start | bytes 294920 | tf_op jit(solution)/shard_map/ppermute | solution.py:15
  49.0 6.7 %collective-permute-start.6 = (f32[768,32]{0,1:T(8,128)S(1)}, f32[768,32]{0,1:T(8,128)S(1)}, u32[]{:S(2)}, u32[]{:S(2)}) collective-permute-start(f32[768,32]{0,1:T(8,128)S(1)} %collective-permute-done.5), channel_id=1, source_target_pairs={{0,2},{2,4},{4,6},{6,8},{8,10},{10,12},{12,14},{14,16},{16,18},{18... | collective-permute-start | bytes 294920 | tf_op jit(solution)/shard_map/ppermute | solution.py:15
  55.8 6.7 %collective-permute-start.7 = (f32[768,32]{0,1:T(8,128)S(1)}, f32[768,32]{0,1:T(8,128)S(1)}, u32[]{:S(2)}, u32[]{:S(2)}) collective-permute-start(f32[768,32]{0,1:T(8,128)S(1)} %collective-permute-done.6), channel_id=1, source_target_pairs={{0,2},{2,4},{4,6},{6,8},{8,10},{10,12},{12,14},{14,16},{16,18},{18... | collective-permute-start | bytes 294920 | tf_op jit(solution)/shard_map/ppermute | solution.py:15
  62.5 6.7 %collective-permute-start.8 = (f32[768,32]{0,1:T(8,128)S(1)}, f32[768,32]{0,1:T(8,128)S(1)}, u32[]{:S(2)}, u32[]{:S(2)}) collective-permute-start(f32[768,32]{0,1:T(8,128)S(1)} %collective-permute-done.7), channel_id=1, source_target_pairs={{0,2},{2,4},{4,6},{6,8},{8,10},{10,12},{12,14},{14,16},{16,18},{18... | collective-permute-start | bytes 294920 | tf_op jit(solution)/shard_map/ppermute | solution.py:15
  69.2 6.7 %collective-permute-start.9 = (f32[768,32]{0,1:T(8,128)S(1)}, f32[768,32]{0,1:T(8,128)S(1)}, u32[]{:S(2)}, u32[]{:S(2)}) collective-permute-start(f32[768,32]{0,1:T(8,128)S(1)} %collective-permute-done.8), channel_id=1, source_target_pairs={{0,2},{2,4},{4,6},{6,8},{8,10},{10,12},{12,14},{14,16},{16,18},{18... | collective-permute-start | bytes 294920 | tf_op jit(solution)/shard_map/ppermute | solution.py:15
  76.0 6.7 %collective-permute-start.10 = (f32[768,32]{0,1:T(8,128)S(1)}, f32[768,32]{0,1:T(8,128)S(1)}, u32[]{:S(2)}, u32[]{:S(2)}) collective-permute-start(f32[768,32]{0,1:T(8,128)S(1)} %collective-permute-done.9), channel_id=1, source_target_pairs={{0,2},{2,4},{4,6},{6,8},{8,10},{10,12},{12,14},{14,16},{16,18},{18... | collective-permute-start | bytes 294920 | tf_op jit(solution)/shard_map/ppermute | solution.py:15
  82.7 6.7 %collective-permute-start.11 = (f32[768,32]{0,1:T(8,128)S(1)}, f32[768,32]{0,1:T(8,128)S(1)}, u32[]{:S(2)}, u32[]{:S(2)}) collective-permute-start(f32[768,32]{0,1:T(8,128)S(1)} %collective-permute-done.10), channel_id=1, source_target_pairs={{0,2},{2,4},{4,6},{6,8},{8,10},{10,12},{12,14},{14,16},{16,18},{18... | collective-permute-start | bytes 294920 | tf_op jit(solution)/shard_map/ppermute | solution.py:15
  89.4 6.7 %collective-permute-start.12 = (f32[768,32]{0,1:T(8,128)S(1)}, f32[768,32]{0,1:T(8,128)S(1)}, u32[]{:S(2)}, u32[]{:S(2)}) collective-permute-start(f32[768,32]{0,1:T(8,128)S(1)} %collective-permute-done.11), channel_id=1, source_target_pairs={{0,2},{2,4},{4,6},{6,8},{8,10},{10,12},{12,14},{14,16},{16,18},{18... | collective-permute-start | bytes 294920 | tf_op jit(solution)/shard_map/ppermute | solution.py:15
  96.2 6.7 %collective-permute-start.13 = (f32[768,32]{0,1:T(8,128)S(1)}, f32[768,32]{0,1:T(8,128)S(1)}, u32[]{:S(2)}, u32[]{:S(2)}) collective-permute-start(f32[768,32]{0,1:T(8,128)S(1)} %collective-permute-done.12), channel_id=1, source_target_pairs={{0,2},{2,4},{4,6},{6,8},{8,10},{10,12},{12,14},{14,16},{16,18},{18... | collective-permute-start | bytes 294920 | tf_op jit(solution)/shard_map/ppermute | solution.py:15
  102.9 6.7 %collective-permute-start.14 = (f32[768,32]{0,1:T(8,128)S(1)}, f32[768,32]{0,1:T(8,128)S(1)}, u32[]{:S(2)}, u32[]{:S(2)}) collective-permute-start(f32[768,32]{0,1:T(8,128)S(1)} %collective-permute-done.13), channel_id=1, source_target_pairs={{0,2},{2,4},{4,6},{6,8},{8,10},{10,12},{12,14},{14,16},{16,18},{18... | collective-permute-start | bytes 294920 | tf_op jit(solution)/shard_map/ppermute | solution.py:15
  103.0 87.8 %reduce-scatter.2.cloned.1.call-start = ((), (), s32[]{:S(2)}) async-start(), calls=%async_computation.3 | async-start | bytes 3145728 | tf_op jit(solution)/shard_map/reduce_scatter | solution.py:23
  130.1 21.8 %copy-start = (f32[1024,768]{1,0:T(8,128)S(1)}, f32[1024,768]{1,0:T(8,128)}, u32[]{:S(2)}) copy-start(f32[1024,768]{1,0:T(8,128)} %param.4) | copy-start | bytes 9437188
Sparse Core Ops, SparseCore 0:
  8.9 35.8 all-gather.2
  103.1 41.2 all-gather.4
  160.1 30.6 reduce-scatter.1
